TPU v7x, 32 devices: a whole 2x2x4 slice. The times are simulated.
32 devices in a mesh: grp: 2 (over y), visit: 16 (over z, x, core).
Axes of the slice: x: 2, y: 2, z: 4, core: 2. Of those that a mesh axis runs over, the one named last changes fastest.
Arguments:
- science: float32 [8192, 1024], P(('grp', 'visit')), parts along dimension 0, may hold values from -6 to 6
- patches: float32 [256, 256, 256], P(('grp', 'visit')), parts along dimension 0, may hold values from -6 to 6
- margin: int32 [128, 3], P('grp'), parts along dimension 0, may hold values from 0 to 255, as said below
- kernel_coef: float32 [27, 128], P(None, ('grp', 'visit')), parts along dimension 1, may hold values from -4 to 4
- ccd_first: int32 [32], P('grp'), parts along dimension 0, may hold values 0 or 1
Outputs:
- patch_mean: float32 [256, 256, 256], P(('grp', 'visit')), parts along dimension 0
There are 2 independent parts, one for each index of `grp`. A program takes and returns all parts, laid end to end along the dimension named above; each array names one. Nothing has to cross between parts.
Inputs may be any that keep to these rules, and one draw needn't show every extreme that they name: `margin`: column 0 is a patch id, columns 1 and 2 are offsets below 256. A tile of strip d names a patch owned by strip d - 1, d or d + 1. Among the 4 tiles of one strip at most 2 name patches of one owner (patch id // 8), and in every strip some owner is named exactly 2 times.
All inputs are finite; a program needn't handle non-finite values.
Results may differ from a plain program's by a relative error of at most 0.004.
Values may be sent and summed in bfloat16 or wider, within the bound.
No kernel may reach another device: no remote copies, remote signals or barrier semaphores. Data moves between devices by JAX's collectives and lax.ppermute only.
A program may use at most 64 MiB of HBM per device.

v0:
```python
import functools

import jax
import jax.numpy as jnp
import numpy as np
from jax import lax
from jax.experimental import pallas as pl
from jax.experimental.pallas import tpu as pltpu
from jax.sharding import PartitionSpec as P

TILE = 256
HALF = 128
RADIUS = 10
SIGMAS = 3
ORDERS = 3
EDGE = 16
CAP = 2
STRIPS = 3
SLOTS = STRIPS * CAP
KINDS = 4
TOP, BOTTOM, LEFT, RIGHT = range(KINDS)
PIECES = SLOTS * KINDS
FRAME_ROWS = PIECES * EDGE
COEF_ROWS = 32


def owned_slots(margin, owner, strips, per_strip, owned):
    slots = []
    for q in range(STRIPS):
        strip = owner - 1 + q
        inside = (strip >= 0) & (strip < strips)
        base = jnp.clip(strip, 0, strips - 1) * per_strip
        count = jnp.int32(0)
        found = [jnp.int32(-1) for _ in range(CAP)]
        for s in range(per_strip):
            mine = inside & (lax.div(margin[(base + s) * 3], owned) == owner)
            for j in range(CAP):
                found[j] = jnp.where(mine & (count == j), base + s, found[j])
            count = count + jnp.where(mine, 1, 0)
        slots.extend(found)
    return slots


def partner_sign(owner):
    return 1 - 2 * lax.rem(owner, 2)


def pack_kernel(sizes, margin, coef, patches, science, aligned, to_chip, to_next, to_far, own_coef,
                patch_buf, science_buf, slot_of, patch_sem, science_sem):
    strips, per_strip, owned = sizes
    owner = lax.axis_index("visit")
    sign = partner_sign(owner)
    slots = owned_slots(margin, owner, strips, per_strip, owned)
    for k in range(SLOTS):
        slot_of[k] = slots[k]

        @pl.when(slots[k] >= 0)
        def _(k=k):
            local = lax.rem(margin[jnp.maximum(slots[k], 0) * 3], owned)
            pltpu.make_async_copy(patches.at[local], patch_buf.at[k], patch_sem.at[k]).start()

    whole = pltpu.make_async_copy(science, science_buf, science_sem)
    whole.start()

    def slot_step(k, carry):
        tile = slot_of[k]

        @pl.when(tile >= 0)
        def _():
            down = margin[tile * 3 + 1]
            right = margin[tile * 3 + 2]
            local = lax.rem(margin[tile * 3], owned)
            pltpu.make_async_copy(patches.at[local], patch_buf.at[k], patch_sem.at[k]).wait()
            moved = pltpu.roll(pltpu.roll(patch_buf[k], down, 0), right, 1)
            moved16 = moved.astype(jnp.bfloat16)
            aligned[k] = moved16
            row = k * KINDS * EDGE
            to_chip[pl.ds(row + TOP * EDGE, EDGE), :] = moved16[:EDGE]
            to_chip[pl.ds(row + BOTTOM * EDGE, EDGE), :] = moved16[TILE - EDGE :]
            left = jnp.transpose(moved[:, :HALF])[:EDGE]
            right_edge = jnp.transpose(moved[:, TILE - HALF :])[HALF - EDGE :]
            to_chip[pl.ds(row + LEFT * EDGE, EDGE), :] = left.astype(jnp.bfloat16)
            to_chip[pl.ds(row + RIGHT * EDGE, EDGE), :] = right_edge.astype(jnp.bfloat16)

        return carry

    lax.fori_loop(0, SLOTS, slot_step, 0)

    @pl.when(sign < 0)
    def _():
        for j in range(CAP):
            source = (((STRIPS - 1) * CAP + j) * KINDS + BOTTOM) * EDGE
            to_far[j * EDGE : (j + 1) * EDGE, :] = to_chip[source : source + EDGE, :]

    @pl.when(sign > 0)
    def _():
        for j in range(CAP):
            source = (j * KINDS + TOP) * EDGE
            to_far[j * EDGE : (j + 1) * EDGE, :] = to_chip[source : source + EDGE, :]

    lane4 = lax.broadcasted_iota(jnp.int32, coef.shape, 1)
    lanes = lax.broadcasted_iota(jnp.int32, (COEF_ROWS, TILE), 1)
    bases = coef.shape[0]
    coefs = coef[...]

    def coef_block(offset):
        block = jnp.zeros((COEF_ROWS, TILE), jnp.float32)
        count = jnp.int32(0)
        for s in range(per_strip):
            tile = owner * per_strip + s
            match = lax.div(margin[tile * 3], owned) == owner + offset
            column = jnp.sum(jnp.where(lane4 == s, coefs, 0.0), axis=1, keepdims=True)
            column = jnp.concatenate([column, jnp.zeros((COEF_ROWS - bases, 1), jnp.float32)], axis=0)
            high = column.astype(jnp.bfloat16).astype(jnp.float32)
            rest = column - high
            middle = rest.astype(jnp.bfloat16).astype(jnp.float32)
            low = rest - middle
            for part, value in enumerate((high, middle, low)):
                block = block + jnp.where(match & (lanes == count * 3 + part), value, 0.0)
            count = count + jnp.where(match, 1, 0)
        return block.astype(jnp.bfloat16)

    own_coef[...] = coef_block(0)
    chip_rows = FRAME_ROWS + CAP * TILE
    to_chip[chip_rows : chip_rows + COEF_ROWS, :] = coef_block(sign)
    to_next[CAP * TILE : CAP * TILE + COEF_ROWS, :] = coef_block(-sign)
    whole.wait()
    for ref, offset, first in ((to_chip, sign, FRAME_ROWS), (to_next, -sign, 0)):
        count = jnp.int32(0)
        for s in range(per_strip):
            match = lax.div(margin[(owner * per_strip + s) * 3], owned) == owner + offset

            @pl.when(match)
            def _(ref=ref, first=first, count=count, s=s):
                start = pl.multiple_of(first + count * TILE, EDGE)
                ref[pl.ds(start, TILE), :] = science_buf[:, s * TILE : (s + 1) * TILE].astype(jnp.bfloat16)

            count = count + jnp.where(match, 1, 0)


def profile(u, sigma, order):
    taps = np.arange(-RADIUS, RADIUS + 1).astype(np.float32)
    total = float(np.sum(np.exp(-taps * taps / np.float32(2.0 * sigma * sigma)), dtype=np.float32))
    shape = jnp.where(jnp.abs(u) <= RADIUS, jnp.exp(-u * u / (2.0 * sigma * sigma)) / total, 0.0)
    for _ in range(order):
        shape = shape * (u / sigma)
    return shape


def match_kernel(sizes, margin, ccd_first, aligned, from_chip, frames_next, science_next, frames_across, from_far,
                 own_frames, own_coef, science, out,
                 frames, aligned_buf, far_buf, science_buf, coefs, local_science, window, spread, mixes, table, across,
                 total, slot_of, sems):
    strips, per_strip, owned = sizes
    owner = lax.axis_index("visit")
    sign = partner_sign(owner)
    copies = [
        (own_frames.at[pl.ds(0, FRAME_ROWS)], frames.at[3]),
        (from_chip.at[pl.ds(0, FRAME_ROWS)], frames.at[4]),
        (frames_next.at[pl.ds(0, FRAME_ROWS)], frames.at[2]),
        (frames_next.at[pl.ds(FRAME_ROWS, FRAME_ROWS)], frames.at[1]),
        (frames_across.at[pl.ds(0, FRAME_ROWS)], frames.at[5]),
        (frames_across.at[pl.ds(FRAME_ROWS, FRAME_ROWS)], frames.at[6]),
        (from_far, far_buf),
        (own_coef, coefs.at[1]),
        (from_chip.at[pl.ds(FRAME_ROWS + CAP * TILE, COEF_ROWS)], coefs.at[2]),
        (science_next.at[pl.ds(CAP * TILE, COEF_ROWS)], coefs.at[0]),
        (from_chip.at[pl.ds(FRAME_ROWS, CAP * TILE)], science_buf.at[1]),
        (science_next.at[pl.ds(0, CAP * TILE)], science_buf.at[0]),
        (science, local_science),
        (aligned, aligned_buf),
    ]
    started = [pltpu.make_async_copy(a, b, sems.at[n]) for n, (a, b) in enumerate(copies)]
    for copy in started:
        copy.start()

    slots = owned_slots(margin, owner, strips, per_strip, owned)
    ids = [jnp.where(t >= 0, margin[jnp.maximum(t, 0) * 3], -1) for t in slots]
    for k in range(SLOTS):
        slot_of[k] = slots[k]
        slot_of[SLOTS + k] = sum(jnp.where(other == ids[k], 1, 0) for other in ids)

    u = (lax.broadcasted_iota(jnp.int32, (HALF, TILE), 1) - lax.broadcasted_iota(jnp.int32, (HALF, TILE), 0) - EDGE)
    u = u.astype(jnp.float32)
    w = lax.broadcasted_iota(jnp.int32, (TILE, HALF), 0) - lax.broadcasted_iota(jnp.int32, (TILE, HALF), 1)
    w = jnp.where(w > HALF, w - TILE, w).astype(jnp.float32)
    for g in range(SIGMAS):
        sigma = 0.75 * 2.0**g
        for k in range(ORDERS):
            n = g * ORDERS + k
            table[n] = profile(u, sigma, k)
            across[:, n * HALF : (n + 1) * HALF] = profile(w, sigma, k).astype(jnp.bfloat16)
    window_rows = TILE + 2 * EDGE
    for n in range(SIGMAS * ORDERS):
        spread[n, window_rows:, :] = jnp.zeros((HALF + TILE - window_rows, TILE), jnp.bfloat16)
    out[...] = jnp.zeros(out.shape, jnp.float32)
    for copy in started:
        copy.wait()
    far_strip = jnp.where(sign > 0, STRIPS - 1, 0)
    far_kind = jnp.where(sign > 0, BOTTOM, TOP)
    for j in range(CAP):
        start = pl.multiple_of(((far_strip * CAP + j) * KINDS + far_kind) * EDGE, EDGE)
        frames[0, pl.ds(start, EDGE), :] = far_buf[j * EDGE : (j + 1) * EDGE, :]

    def piece(strip, position, kind, allowed):
        inside = (strip >= 0) & (strip < strips) & (position >= 0) & (position < per_strip) & allowed
        base = jnp.clip(strip, 0, strips - 1) * per_strip
        where = jnp.clip(position, 0, per_strip - 1)
        its_owner = lax.div(margin[(base + where) * 3], owned)
        rank = jnp.int32(0)
        for s in range(per_strip):
            same = lax.div(margin[(base + s) * 3], owned) == its_owner
            rank = rank + jnp.where(same & (s < where), 1, 0)
        relative = jnp.clip(strip, 0, strips - 1) - its_owner + 1
        member = jnp.clip((its_owner - owner) * sign + 3, 0, 6)
        row = jnp.clip((relative * CAP + rank) * KINDS + kind, 0, PIECES - 1) * EDGE
        value = frames[member, pl.ds(pl.multiple_of(row, EDGE), EDGE), :]
        return jnp.where(inside, value, jnp.zeros_like(value))

    def slot_step(k, carry):
        tile = slot_of[k]

        @pl.when(tile >= 0)
        def _():
            q = lax.div(k, CAP)
            j = lax.rem(k, CAP)
            strip = owner - 1 + q
            position = tile - strip * per_strip
            down = margin[tile * 3 + 1]
            right = margin[tile * 3 + 2]
            local = lax.rem(margin[tile * 3], owned)
            yes = owner >= 0
            keep_top = (strip > 0) & (ccd_first[strip] == 0)
            keep_bottom = (strip < strips - 1) & (ccd_first[jnp.minimum(strip + 1, strips - 1)] == 0)

            from_right = piece(strip, position + 1, LEFT, yes).astype(jnp.float32)
            from_left = piece(strip, position - 1, RIGHT, yes).astype(jnp.float32)
            sides = jnp.concatenate(
                [from_right, jnp.zeros((HALF - 2 * EDGE, TILE), jnp.float32), from_left], axis=0
            )
            sides = jnp.transpose(sides).astype(jnp.bfloat16)

            def place(first, rows, middle_a, middle_b, left_b, right_a):
                low = lax.broadcasted_iota(jnp.int32, (rows, HALF), 1) < HALF // 2
                window[0, first : first + rows, :HALF] = middle_a
                window[0, first : first + rows, HALF:] = jnp.where(low, middle_b, left_b)
                window[1, first : first + rows, :HALF] = middle_b
                window[1, first : first + rows, HALF:] = jnp.where(low, right_a, middle_a)

            center = aligned_buf[k]
            place(EDGE, TILE, center[:, :HALF], center[:, HALF:], sides, sides)
            for first, neighbour, kind, keep in (
                (0, strip - 1, BOTTOM, keep_top),
                (EDGE + TILE, strip + 1, TOP, keep_bottom),
            ):
                middle = piece(neighbour, position, kind, keep)
                left = piece(neighbour, position - 1, kind, keep)
                right_piece = piece(neighbour, position + 1, kind, keep)
                place(first, EDGE, middle[:, :HALF], middle[:, HALF:], left[:, HALF:], right_piece[:, :HALF])

            columns = SIGMAS * ORDERS
            for c in range(2):
                for n in range(0, columns, 2):
                    wide = min(2, columns - n)
                    h = jnp.dot(
                        window[c], across[:, n * HALF : (n + wide) * HALF], preferred_element_type=jnp.float32
                    ).astype(jnp.bfloat16)
                    for m in range(wide):
                        spread[n + m, :window_rows, c * HALF : (c + 1) * HALF] = h[:, m * HALF : (m + 1) * HALF]

            member = (q - 1) * sign + 1
            block = coefs[member].astype(jnp.float32)
            lanes = lax.broadcasted_iota(jnp.int32, block.shape, 1)
            mine = (lanes >= j * 3) & (lanes < j * 3 + 3)
            column = jnp.sum(jnp.where(mine, block, 0.0), axis=1, keepdims=True)
            for g in range(SIGMAS):
                for h in range(ORDERS):
                    mix = jnp.zeros((HALF, TILE), jnp.float32)
                    for v in range(ORDERS):
                        n = (g * ORDERS + h) * ORDERS + v
                        mix = mix + column[n : n + 1, :] * table[g * ORDERS + v]
                    mixes[g * ORDERS + h] = mix.astype(jnp.bfloat16)
            for r in range(2):
                acc = jnp.zeros((HALF, TILE), jnp.float32)
                for n in range(columns):
                    acc = acc + jnp.dot(
                        mixes[n], spread[n, r * HALF : r * HALF + TILE, :], preferred_element_type=jnp.float32
                    )
                total[r * HALF : (r + 1) * HALF, :] = acc

            @pl.when(q == 1)
            def _():
                start = pl.multiple_of(position * TILE, TILE)
                total[...] = local_science[:, pl.ds(start, TILE)] - total[...]

            @pl.when(q != 1)
            def _():
                start = pl.multiple_of(j * TILE, TILE)
                arrived = science_buf[lax.div(member, 2), pl.ds(start, TILE), :]
                total[...] = arrived.astype(jnp.float32) - total[...]

            back = pltpu.roll(pltpu.roll(total[...], lax.rem(TILE - down, TILE), 0), lax.rem(TILE - right, TILE), 1)
            count = slot_of[SLOTS + k]
            share = jnp.float32(1.0)
            for n in range(2, SLOTS + 1):
                share = jnp.where(count == n, jnp.float32(1.0 / n), share)
            out[local] = out[local] + back * share

        return carry

    lax.fori_loop(0, SLOTS, slot_step, 0)


def body(science, patches, margin, kernel_coef, ccd_first):
    strips = lax.axis_size("visit")
    owned = patches.shape[0]
    per_strip = science.shape[1] // TILE
    sizes = (strips, per_strip, owned)
    flat = margin.reshape(-1)
    smem = pl.BlockSpec(memory_space=pltpu.SMEM)
    vmem = pl.BlockSpec(memory_space=pltpu.VMEM)
    hbm = pl.BlockSpec(memory_space=pl.ANY)
    bf16 = jnp.bfloat16
    f32 = jnp.float32
    chip_rows = FRAME_ROWS + CAP * TILE + COEF_ROWS
    next_rows = CAP * TILE + COEF_ROWS
    far_rows = CAP * EDGE
    aligned, to_chip, to_next, to_far, own_coef = pl.pallas_call(
        functools.partial(pack_kernel, sizes),
        out_shape=(
            jax.ShapeDtypeStruct((SLOTS, TILE, TILE), bf16),
            jax.ShapeDtypeStruct((chip_rows, TILE), bf16),
            jax.ShapeDtypeStruct((next_rows, TILE), bf16),
            jax.ShapeDtypeStruct((far_rows, TILE), bf16),
            jax.ShapeDtypeStruct((COEF_ROWS, TILE), bf16),
        ),
        in_specs=[smem, vmem, hbm, hbm],
        out_specs=(vmem, vmem, vmem, vmem, vmem),
        scratch_shapes=[
            pltpu.VMEM((SLOTS, TILE, TILE), f32),
            pltpu.VMEM((TILE, per_strip * TILE), f32),
            pltpu.SMEM((SLOTS,), jnp.int32),
            pltpu.SemaphoreType.DMA((SLOTS,)),
            pltpu.SemaphoreType.DMA,
        ],
        name="pack",
    )(flat, kernel_coef, patches, science)

    on_chip = [(i, i ^ 1) for i in range(strips)]
    next_chip = [p for i in range(1, strips - 1, 2) for p in ((i, i + 1), (i + 1, i))]
    far = [p for i in range(1, strips - 3, 2) for p in ((i, i + 3), (i + 3, i))]
    from_far = lax.ppermute(to_far, "visit", far)
    from_chip = lax.ppermute(to_chip, "visit", on_chip)
    both = jnp.concatenate([to_chip[:FRAME_ROWS], from_chip[:FRAME_ROWS]], axis=0)
    frames_next = lax.ppermute(both, "visit", next_chip)
    science_next = lax.ppermute(to_next, "visit", next_chip)
    frames_across = lax.ppermute(frames_next, "visit", on_chip)

    columns = SIGMAS * ORDERS
    return pl.pallas_call(
        functools.partial(match_kernel, sizes),
        out_shape=jax.ShapeDtypeStruct(patches.shape, f32),
        in_specs=[smem, smem] + [hbm] * 9,
        out_specs=vmem,
        scratch_shapes=[
            pltpu.VMEM((7, FRAME_ROWS, TILE), bf16),
            pltpu.VMEM((SLOTS, TILE, TILE), bf16),
            pltpu.VMEM((far_rows, TILE), bf16),
            pltpu.VMEM((2, CAP * TILE, TILE), bf16),
            pltpu.VMEM((3, COEF_ROWS, TILE), bf16),
            pltpu.VMEM((TILE, per_strip * TILE), f32),
            pltpu.VMEM((2, TILE + 2 * EDGE, TILE), bf16),
            pltpu.VMEM((columns, TILE + HALF, TILE), bf16),
            pltpu.VMEM((columns, HALF, TILE), bf16),
            pltpu.VMEM((columns, HALF, TILE), f32),
            pltpu.VMEM((TILE, columns * HALF), bf16),
            pltpu.VMEM((TILE, TILE), f32),
            pltpu.SMEM((2 * SLOTS,), jnp.int32),
            pltpu.SemaphoreType.DMA((14,)),
        ],
        name="match",
    )(flat, ccd_first, aligned, from_chip, frames_next, science_next, frames_across, from_far, to_chip, own_coef, science)


def solution(mesh):
    in_specs = (
        P(("grp", "visit"), None),
        P(("grp", "visit"), None, None),
        P("grp", None),
        P(None, ("grp", "visit")),
        P("grp"),
    )
    out_specs = P(("grp", "visit"), None, None)
    return jax.shard_map(body, mesh=mesh, in_specs=in_specs, out_specs=out_specs, check_vma=False)
```

profile of v0, /device:TPU:15, one launch (start us, length us, event | category | flops | bytes accessed | tf_op | source)
XLA Modules:
  0.0 45.3 jit_solution(16493364710642855796)
XLA Ops:
  0.0 1.4 %copy.8.coef = f32[27,4]{1,0:T(8,128)} copy(f32[27,4]{0,1:T(4,128)} %param.8) | data formatting | bytes 864 | tf_op args[3]
  1.4 0.8 %copy.7 = s32[64,3]{1,0:T(8,128)S(1)} copy(s32[64,3]{0,1:T(4,128)} %param.7) | data formatting | bytes 1536 | tf_op args[2]
  2.1 0.7 %reshape.3.margin = s32[192]{0:T(256)} reshape(s32[64,3]{1,0:T(8,128)S(1)} %copy.7) | data formatting | bytes 1536 | tf_op jit(solution)/shard_map/reshape | solution.py:319
  2.9 4.8 %pack.1 = (bf16[6,256,256]{2,1,0:T(8,128)(2,1)}, bf16[928,256]{1,0:T(8,128)(2,1)}, bf16[544,256]{1,0:T(8,128)(2,1)}, bf16[32,256]{1,0:T(8,128)(2,1)}, bf16[32,256]{1,0:T(8,128)(2,1)}) custom-call(s32[192]{0:T(256)} %reshape.3.margin, f32[27,4]{1,0:T(8,128)} %copy.8.coef, f32[8,256,256]{2,1,0:T(8,128)} %patches.1, f32[256,1024]{1,0:T(8,128)} %science.3), custom_call_target="tpu_custom_call" | custom-call | tf_op jit(solution)/shard_map/pack/pallas_call | solution.py:328
  7.7 0.3 collective-permute-start
  8.0 0.9 %slice.6 = bf16[384,256]{1,0:T(8,128)(2,1)S(1)} slice(bf16[928,256]{1,0:T(8,128)(2,1)} %get-tuple-element.11.own_frames), slice={[0:384], [0:256]} | slice | bytes 393216 | tf_op jit(solution)/shard_map/slice | solution.py:354
  8.9 0.9 %collective-permute-done.from_chip = bf16[928,256]{1,0:T(8,128)(2,1)S(1)} collective-permute-done((bf16[928,256]{1,0:T(8,128)(2,1)}, bf16[928,256]{1,0:T(8,128)(2,1)S(1)}, u32[]{:S(2)}, u32[]{:S(2)}) %collective-permute-start) | collective-permute-done | bytes 475168 | tf_op jit(solution)/shard_map/ppermute | solution.py:353
  9.8 0.0 copy-start
  9.9 3.3 %collective-permute-start.1 = (bf16[768,256]{1,0:T(8,128)(2,1)S(1)}, bf16[768,256]{1,0:T(8,128)(2,1)S(1)}, u32[]{:S(2)}, u32[]{:S(2)}) collective-permute-start(bf16[768,256]{1,0:T(8,128)(2,1)S(1)} %pad_maximum_fusion), channel_id=1, source_target_pairs={{1,2},{2,1},{3,4},{4,3},{5,6},{6,5},{7,8},{8,7},{9,10},{10,9},{11,... | collective-permute-start | bytes 1179656 | tf_op jit(solution)/shard_map/ppermute | solution.py:355
  13.2 6.8 %collective-permute-done.1.frames_next = bf16[768,256]{1,0:T(8,128)(2,1)S(1)} collective-permute-done((bf16[768,256]{1,0:T(8,128)(2,1)S(1)}, bf16[768,256]{1,0:T(8,128)(2,1)S(1)}, u32[]{:S(2)}, u32[]{:S(2)}) %collective-permute-start.1) | collective-permute-done | bytes 393248 | tf_op jit(solution)/shard_map/ppermute | solution.py:355
  20.0 0.0 copy-start.1
  20.0 3.4 %collective-permute-start.3 = (bf16[768,256]{1,0:T(8,128)(2,1)S(1)}, bf16[768,256]{1,0:T(8,128)(2,1)S(1)}, u32[]{:S(2)}, u32[]{:S(2)}) collective-permute-start(bf16[768,256]{1,0:T(8,128)(2,1)S(1)} %collective-permute-done.1.frames_next), channel_id=1, source_target_pairs={{0,1},{1,0},{2,3},{3,2},{4,5},{5,4},{6,7},{7,6},{8,9},{9,8},{10,11... | collective-permute-start | bytes 1179656 | tf_op jit(solution)/shard_map/ppermute | solution.py:357
  23.4 3.2 %collective-permute-start.2 = (bf16[544,256]{1,0:T(8,128)(2,1)}, bf16[544,256]{1,0:T(8,128)(2,1)S(1)}, u32[]{:S(2)}, u32[]{:S(2)}) collective-permute-start(bf16[544,256]{1,0:T(8,128)(2,1)} %get-tuple-element.12), channel_id=1, source_target_pairs={{1,2},{2,1},{3,4},{4,3},{5,6},{6,5},{7,8},{8,7},{9,10},{10,9},{11,... | collective-permute-start | bytes 835592 | tf_op jit(solution)/shard_map/ppermute | solution.py:356
  26.6 2.1 %collective-permute-start.4 = (bf16[32,256]{1,0:T(8,128)(2,1)}, bf16[32,256]{1,0:T(8,128)(2,1)S(1)}, u32[]{:S(2)}, u32[]{:S(2)}) collective-permute-start(bf16[32,256]{1,0:T(8,128)(2,1)} %get-tuple-element.13), channel_id=1, source_target_pairs={{1,4},{4,1},{3,6},{6,3},{5,8},{8,5},{7,10},{10,7},{9,12},{12,9},{1... | collective-permute-start | bytes 49160 | tf_op jit(solution)/shard_map/ppermute | solution.py:352
  28.7 3.5 %collective-permute-done.4.from_far = bf16[32,256]{1,0:T(8,128)(2,1)S(1)} collective-permute-done((bf16[32,256]{1,0:T(8,128)(2,1)}, bf16[32,256]{1,0:T(8,128)(2,1)S(1)}, u32[]{:S(2)}, u32[]{:S(2)}) %collective-permute-start.4) | collective-permute-done | bytes 16416 | tf_op jit(solution)/shard_map/ppermute | solution.py:352
  32.2 0.0 copy-start.4
  32.2 0.3 collective-permute-done.2.science_next
  32.4 0.0 copy-start.3
  32.4 0.0 collective-permute-done.3.frames_across
  32.4 0.0 copy-start.2
  32.4 0.0 copy-done
  32.5 0.0 copy-done.1
  32.5 0.3 copy-done.4
  32.8 0.4 copy-done.3
  33.2 0.1 copy-done.2
  33.3 12.0 %match.1 = f32[8,256,256]{2,1,0:T(8,128)} custom-call(s32[192]{0:T(256)} %reshape.3.margin, s32[16]{0:T(128)} %ccd_first.1, bf16[6,256,256]{2,1,0:T(8,128)(2,1)} %get-tuple-element.10.aligned, bf16[928,256]{1,0:T(8,128)(2,1)} %copy-done, bf16[768,256]{1,0:T(8,128)(2,1)} %copy-done.1, bf16[544,256]{1,0:T(8,128)(2,1)} %copy-done.3, ...), custom_call_target="tpu_custom_call" | custom-call | tf_op jit(solution)/shard_map/match/pallas_call | solution.py:360
  (2 shorter events, 0.0 us)
Async XLA Ops:
  7.7 2.1 %collective-permute-start = (bf16[928,256]{1,0:T(8,128)(2,1)}, bf16[928,256]{1,0:T(8,128)(2,1)S(1)}, u32[]{:S(2)}, u32[]{:S(2)}) collective-permute-start(bf16[928,256]{1,0:T(8,128)(2,1)} %get-tuple-element.11.own_frames), channel_id=1, source_target_pairs={{0,1},{1,0},{2,3},{3,2},{4,5},{5,4},{6,7},{7,6},{8,9},{9,8},{10,11... | collective-permute-start | bytes 1425416 | tf_op jit(solution)/shard_map/ppermute | solution.py:353
  9.8 22.6 %copy-start = (bf16[928,256]{1,0:T(8,128)(2,1)}, bf16[928,256]{1,0:T(8,128)(2,1)S(1)}, u32[]{:S(2)}) copy-start(bf16[928,256]{1,0:T(8,128)(2,1)S(1)} %collective-permute-done.from_chip) | copy-start | bytes 1425412
  9.9 10.1 %collective-permute-start.1 = (bf16[768,256]{1,0:T(8,128)(2,1)S(1)}, bf16[768,256]{1,0:T(8,128)(2,1)S(1)}, u32[]{:S(2)}, u32[]{:S(2)}) collective-permute-start(bf16[768,256]{1,0:T(8,128)(2,1)S(1)} %pad_maximum_fusion), channel_id=1, source_target_pairs={{1,2},{2,1},{3,4},{4,3},{5,6},{6,5},{7,8},{8,7},{9,10},{10,9},{11,... | collective-permute-start | bytes 1179656 | tf_op jit(solution)/shard_map/ppermute | solution.py:355
  20.0 12.5 %copy-start.1 = (bf16[768,256]{1,0:T(8,128)(2,1)}, bf16[768,256]{1,0:T(8,128)(2,1)S(1)}, u32[]{:S(2)}) copy-start(bf16[768,256]{1,0:T(8,128)(2,1)S(1)} %collective-permute-done.1.frames_next) | copy-start | bytes 1179652
  20.0 12.5 %collective-permute-start.3 = (bf16[768,256]{1,0:T(8,128)(2,1)S(1)}, bf16[768,256]{1,0:T(8,128)(2,1)S(1)}, u32[]{:S(2)}, u32[]{:S(2)}) collective-permute-start(bf16[768,256]{1,0:T(8,128)(2,1)S(1)} %collective-permute-done.1.frames_next), channel_id=1, source_target_pairs={{0,1},{1,0},{2,3},{3,2},{4,5},{5,4},{6,7},{7,6},{8,9},{9,8},{10,11... | collective-permute-start | bytes 1179656 | tf_op jit(solution)/shard_map/ppermute | solution.py:357
  23.4 9.1 %collective-permute-start.2 = (bf16[544,256]{1,0:T(8,128)(2,1)}, bf16[544,256]{1,0:T(8,128)(2,1)S(1)}, u32[]{:S(2)}, u32[]{:S(2)}) collective-permute-start(bf16[544,256]{1,0:T(8,128)(2,1)} %get-tuple-element.12), channel_id=1, source_target_pairs={{1,2},{2,1},{3,4},{4,3},{5,6},{6,5},{7,8},{8,7},{9,10},{10,9},{11,... | collective-permute-start | bytes 835592 | tf_op jit(solution)/shard_map/ppermute | solution.py:356
  26.6 5.6 %collective-permute-start.4 = (bf16[32,256]{1,0:T(8,128)(2,1)}, bf16[32,256]{1,0:T(8,128)(2,1)S(1)}, u32[]{:S(2)}, u32[]{:S(2)}) collective-permute-start(bf16[32,256]{1,0:T(8,128)(2,1)} %get-tuple-element.13), channel_id=1, source_target_pairs={{1,4},{4,1},{3,6},{6,3},{5,8},{8,5},{7,10},{10,7},{9,12},{12,9},{1... | collective-permute-start | bytes 49160 | tf_op jit(solution)/shard_map/ppermute | solution.py:352
  32.2 0.6 %copy-start.4 = (bf16[32,256]{1,0:T(8,128)(2,1)}, bf16[32,256]{1,0:T(8,128)(2,1)S(1)}, u32[]{:S(2)}) copy-start(bf16[32,256]{1,0:T(8,128)(2,1)S(1)} %collective-permute-done.4.from_far) | copy-start | bytes 49156
  32.4 0.7 %copy-start.3 = (bf16[544,256]{1,0:T(8,128)(2,1)}, bf16[544,256]{1,0:T(8,128)(2,1)S(1)}, u32[]{:S(2)}) copy-start(bf16[544,256]{1,0:T(8,128)(2,1)S(1)} %collective-permute-done.2.science_next) | copy-start | bytes 835588
  32.4 0.8 %copy-start.2 = (bf16[768,256]{1,0:T(8,128)(2,1)}, bf16[768,256]{1,0:T(8,128)(2,1)S(1)}, u32[]{:S(2)}) copy-start(bf16[768,256]{1,0:T(8,128)(2,1)S(1)} %collective-permute-done.3.frames_across) | copy-start | bytes 1179652
where the time goes:
time: 46.2 us; the launch traced here: 45.3 us
  Pallas kernels  16.9 us (37%)
  starting transfers between devices  12.3 us (27%)
  waiting for transfers between devices  11.4 us (25%)
  local copies, waits for them, and re-layouts  4.63 us (10%)
    pallas_call x1, Pallas kernels, body(): pl.pallas_call(functools.partial(match_kernel, sizes), out_shape=jax.Shap...  12 us
    ppermute x1, waiting for transfers between devices, body(): frames_next = lax.ppermute(both, 'visit', next_chip)  6.79 us
    pallas_call x1, Pallas kernels, body(): pl.pallas_call(functools.partial(pack_kernel, sizes), out_shape=(jax.Shap...  4.83 us
    ppermute x1, waiting for transfers between devices, body(): from_far = lax.ppermute(to_far, 'visit', far)  3.48 us
    ppermute x1, starting transfers between devices, body(): frames_across = lax.ppermute(frames_next, 'visit', on_chip)  3.42 us
    ppermute x1, starting transfers between devices, body(): frames_next = lax.ppermute(both, 'visit', next_chip)  3.3 us
    ppermute x1, starting transfers between devices, body(): science_next = lax.ppermute(to_next, 'visit', next_chip)  3.22 us
    unnamed x12, local copies, waits for them, and re-layouts  2.97 us
  transfers between devices with their start and end apart: 5, of which 4 were waited for; matrix products, arithmetic and copies ran while one was open for 2% of the time, Pallas kernels for 0%

commit v1 on v0

v1 whole, which is shorter than its diff:
```python
import functools

import jax
import jax.numpy as jnp
import numpy as np
from jax import lax
from jax.experimental import pallas as pl
from jax.experimental.pallas import tpu as pltpu
from jax.sharding import PartitionSpec as P

TILE = 256
HALF = 128
RADIUS = 10
SIGMAS = 3
ORDERS = 3
EDGE = 16
CAP = 2
STRIPS = 3
SLOTS = STRIPS * CAP
KINDS = 4
TOP, BOTTOM, LEFT, RIGHT = range(KINDS)
PIECES = SLOTS * KINDS
COEF_ROWS = 16
NEAR = 8
PIECE_ROWS = CAP * EDGE
NEAR_ROWS = COEF_ROWS + NEAR * PIECE_ROWS
RECORD = COEF_ROWS + PIECES * EDGE


def owned_slots(margin, owner, strips, per_strip, owned):
    slots = []
    for q in range(STRIPS):
        strip = owner - 1 + q
        inside = (strip >= 0) & (strip < strips)
        base = jnp.clip(strip, 0, strips - 1) * per_strip
        count = jnp.int32(0)
        found = [jnp.int32(-1) for _ in range(CAP)]
        for s in range(per_strip):
            mine = inside & (lax.div(margin[0, base + s], owned) == owner)
            for j in range(CAP):
                found[j] = jnp.where(mine & (count == j), base + s, found[j])
            count = count + jnp.where(mine, 1, 0)
        slots.extend(found)
    return slots


def sign_of(owner):
    return 1 - 2 * lax.rem(owner, 2)


def piece_position(relative, kind, sign):
    along = relative * sign
    facing = jnp.where(sign > 0, kind, jnp.where(kind == TOP, BOTTOM, jnp.where(kind == BOTTOM, TOP, kind)))
    middle = jnp.where(facing == TOP, 4, jnp.where(facing == BOTTOM, 11, facing + 3))
    return jnp.where(along < 0, facing, jnp.where(along > 0, 7 + facing, middle))


def pack_kernel(sizes, margin_hbm, coef_hbm, patches, science, aligned, to_chip, to_next, to_far,
                margin, coef, patch_buf, science_buf, slot_of, patch_sem, science_sem, small_sem):
    strips, per_strip, owned = sizes
    tables = [
        pltpu.make_async_copy(a, b, small_sem.at[n]) for n, (a, b) in enumerate(((margin_hbm, margin), (coef_hbm, coef)))
    ]
    for copy in tables:
        copy.start()
    whole = pltpu.make_async_copy(science, science_buf, science_sem)
    whole.start()
    for copy in tables:
        copy.wait()
    owner = lax.axis_index("visit")
    sign = sign_of(owner)
    slots = owned_slots(margin, owner, strips, per_strip, owned)
    for k in range(SLOTS):
        slot_of[k] = slots[k]

        @pl.when(slots[k] >= 0)
        def _(k=k):
            local = lax.rem(margin[0, jnp.maximum(slots[k], 0)], owned)
            pltpu.make_async_copy(patches.at[local], patch_buf.at[k], patch_sem.at[k]).start()

    values = coef[...]
    bases = values.shape[1]
    high = values.astype(jnp.bfloat16).astype(jnp.float32)
    middle = (values - high).astype(jnp.bfloat16).astype(jnp.float32)
    low = values - high - middle
    parts = jnp.concatenate([high, middle, low, jnp.zeros_like(low)], axis=0).astype(jnp.bfloat16)
    to_chip[:COEF_ROWS, :bases] = parts
    to_next[:COEF_ROWS, :bases] = parts

    def slot_step(k, carry):
        tile = slot_of[k]

        @pl.when(tile >= 0)
        def _():
            down = margin[1, tile]
            right = margin[2, tile]
            local = lax.rem(margin[0, tile], owned)
            pltpu.make_async_copy(patches.at[local], patch_buf.at[k], patch_sem.at[k]).wait()
            moved = pltpu.roll(pltpu.roll(patch_buf[k], down, 0), right, 1)
            moved16 = moved.astype(jnp.bfloat16)
            aligned[k] = moved16
            relative = lax.div(k, CAP) - 1
            j = lax.rem(k, CAP)
            left = jnp.transpose(moved[:, :HALF])[:EDGE]
            right_edge = jnp.transpose(moved[:, TILE - HALF :])[HALF - EDGE :]
            edges = (moved16[:EDGE], moved16[TILE - EDGE :], left.astype(jnp.bfloat16), right_edge.astype(jnp.bfloat16))
            for kind in range(KINDS):
                position = piece_position(relative, jnp.int32(kind), sign)
                row = pl.multiple_of(COEF_ROWS + (position * CAP + j) * EDGE, EDGE)
                to_chip[pl.ds(row, EDGE), :] = edges[kind]

                @pl.when(position < NEAR)
                def _(kind=kind, row=row):
                    to_next[pl.ds(row, EDGE), :] = edges[kind]

                @pl.when(position == 0)
                def _(kind=kind):
                    to_far[pl.ds(pl.multiple_of(j * EDGE, EDGE), EDGE), :] = edges[kind]

        return carry

    lax.fori_loop(0, SLOTS, slot_step, 0)
    whole.wait()
    counts = [jnp.int32(0), jnp.int32(0)]
    for s in range(per_strip):
        tile = owner * per_strip + s
        offset = lax.div(margin[0, tile], owned) - owner

        @pl.when(offset != 0)
        def _(s=s, tile=tile, offset=offset, counts=tuple(counts)):
            up = lax.rem(TILE - margin[1, tile], TILE)
            back = lax.rem(TILE - margin[2, tile], TILE)
            moved = pltpu.roll(pltpu.roll(science_buf[:, s * TILE : (s + 1) * TILE], up, 0), back, 1)
            moved16 = moved.astype(jnp.bfloat16)

            @pl.when(offset == sign)
            def _():
                to_chip[pl.ds(pl.multiple_of(RECORD + counts[0] * TILE, EDGE), TILE), :] = moved16

            @pl.when(offset != sign)
            def _():
                to_next[pl.ds(pl.multiple_of(NEAR_ROWS + counts[1] * TILE, EDGE), TILE), :] = moved16

        counts[0] = counts[0] + jnp.where(offset == sign, 1, 0)
        counts[1] = counts[1] + jnp.where(offset == -sign, 1, 0)


def profile(u, sigma, order):
    taps = np.arange(-RADIUS, RADIUS + 1).astype(np.float32)
    total = float(np.sum(np.exp(-taps * taps / np.float32(2.0 * sigma * sigma)), dtype=np.float32))
    shape = jnp.where(jnp.abs(u) <= RADIUS, jnp.exp(-u * u / (2.0 * sigma * sigma)) / total, 0.0)
    for _ in range(order):
        shape = shape * (u / sigma)
    return shape


def match_kernel(sizes, margin, ccd_first, aligned, own_record, from_chip, from_next, from_two, from_across, from_far,
                 science, out,
                 frames, window, spread, mixes, table, across, total, slot_of):
    strips, per_strip, owned = sizes
    owner = lax.axis_index("visit")
    sign = sign_of(owner)
    near = pl.ds(0, NEAR_ROWS)
    relayed = pl.ds(NEAR_ROWS, RECORD - NEAR_ROWS)
    frames[3] = own_record[:RECORD, :]
    frames[4] = from_chip[:RECORD, :]
    frames[2, near] = from_next[near, :]
    frames[1, relayed] = from_two[...]
    frames[5, near] = from_across[near, :]
    frames[6, relayed] = from_across[relayed, :]
    frames[0, pl.ds(COEF_ROWS, PIECE_ROWS)] = from_far[...]

    slots = owned_slots(margin, owner, strips, per_strip, owned)
    ids = [jnp.where(t >= 0, margin[0, jnp.maximum(t, 0)], -1) for t in slots]
    for k in range(SLOTS):
        slot_of[k] = slots[k]
        slot_of[SLOTS + k] = sum(jnp.where(other == ids[k], 1, 0) for other in ids)

    u = (lax.broadcasted_iota(jnp.int32, (HALF, TILE), 1) - lax.broadcasted_iota(jnp.int32, (HALF, TILE), 0) - EDGE)
    u = u.astype(jnp.float32)
    w = lax.broadcasted_iota(jnp.int32, (TILE, HALF), 0) - lax.broadcasted_iota(jnp.int32, (TILE, HALF), 1)
    w = jnp.where(w > HALF, w - TILE, w).astype(jnp.float32)
    for g in range(SIGMAS):
        sigma = 0.75 * 2.0**g
        for k in range(ORDERS):
            n = g * ORDERS + k
            table[n] = profile(u, sigma, k)
            across[:, n * HALF : (n + 1) * HALF] = profile(w, sigma, k).astype(jnp.bfloat16)
    window_rows = TILE + 2 * EDGE
    for n in range(SIGMAS * ORDERS):
        spread[n, window_rows:, :] = jnp.zeros((HALF + TILE - window_rows, TILE), jnp.bfloat16)
    out[...] = jnp.zeros(out.shape, jnp.float32)
    def piece(strip, position, kind, allowed):
        inside = (strip >= 0) & (strip < strips) & (position >= 0) & (position < per_strip) & allowed
        base = jnp.clip(strip, 0, strips - 1) * per_strip
        where = jnp.clip(position, 0, per_strip - 1)
        its_owner = lax.div(margin[0, base + where], owned)
        rank = jnp.int32(0)
        for s in range(per_strip):
            same = lax.div(margin[0, base + s], owned) == its_owner
            rank = rank + jnp.where(same & (s < where), 1, 0)
        relative = jnp.clip(strip, 0, strips - 1) - its_owner
        member = jnp.clip((its_owner - owner) * sign + 3, 0, 6)
        place = piece_position(relative, jnp.int32(kind), sign_of(its_owner)) * CAP + rank
        row = COEF_ROWS + jnp.clip(place, 0, PIECES - 1) * EDGE
        value = frames[member, pl.ds(pl.multiple_of(row, EDGE), EDGE), :]
        return jnp.where(inside, value, jnp.zeros_like(value))

    def slot_step(k, carry):
        tile = slot_of[k]

        @pl.when(tile >= 0)
        def _():
            q = lax.div(k, CAP)
            j = lax.rem(k, CAP)
            strip = owner - 1 + q
            position = tile - strip * per_strip
            down = margin[1, tile]
            right = margin[2, tile]
            local = lax.rem(margin[0, tile], owned)
            yes = owner >= 0
            keep_top = (strip > 0) & (ccd_first[strip] == 0)
            keep_bottom = (strip < strips - 1) & (ccd_first[jnp.minimum(strip + 1, strips - 1)] == 0)

            from_right = piece(strip, position + 1, LEFT, yes).astype(jnp.float32)
            from_left = piece(strip, position - 1, RIGHT, yes).astype(jnp.float32)
            sides = jnp.concatenate(
                [from_right, jnp.zeros((HALF - 2 * EDGE, TILE), jnp.float32), from_left], axis=0
            )
            sides = jnp.transpose(sides).astype(jnp.bfloat16)

            def place(first, rows, middle_a, middle_b, left_b, right_a):
                low = lax.broadcasted_iota(jnp.int32, (rows, HALF), 1) < HALF // 2
                window[0, first : first + rows, :HALF] = middle_a
                window[0, first : first + rows, HALF:] = jnp.where(low, middle_b, left_b)
                window[1, first : first + rows, :HALF] = middle_b
                window[1, first : first + rows, HALF:] = jnp.where(low, right_a, middle_a)

            center = aligned[k]
            place(EDGE, TILE, center[:, :HALF], center[:, HALF:], sides, sides)
            for first, neighbour, kind, keep in (
                (0, strip - 1, BOTTOM, keep_top),
                (EDGE + TILE, strip + 1, TOP, keep_bottom),
            ):
                middle = piece(neighbour, position, kind, keep)
                left = piece(neighbour, position - 1, kind, keep)
                right_piece = piece(neighbour, position + 1, kind, keep)
                place(first, EDGE, middle[:, :HALF], middle[:, HALF:], left[:, HALF:], right_piece[:, :HALF])

            columns = SIGMAS * ORDERS
            for c in range(2):
                for n in range(0, columns, 2):
                    wide = min(2, columns - n)
                    h = jnp.dot(
                        window[c], across[:, n * HALF : (n + wide) * HALF], preferred_element_type=jnp.float32
                    ).astype(jnp.bfloat16)
                    for m in range(wide):
                        spread[n + m, :window_rows, c * HALF : (c + 1) * HALF] = h[:, m * HALF : (m + 1) * HALF]

            member = (q - 1) * sign
            block = frames[member + 3, :COEF_ROWS, :HALF].astype(jnp.float32)
            rows = lax.broadcasted_iota(jnp.int32, block.shape, 0)
            mine = (lax.rem(rows, per_strip) == position) & (rows < 3 * per_strip)
            weights = jnp.sum(jnp.where(mine, block, 0.0), axis=0, keepdims=True)
            for g in range(SIGMAS):
                for h in range(ORDERS):
                    mix = jnp.zeros((HALF, TILE), jnp.float32)
                    for v in range(ORDERS):
                        n = (g * ORDERS + h) * ORDERS + v
                        mix = mix + weights[:, n : n + 1] * table[g * ORDERS + v]
                    mixes[g * ORDERS + h] = mix.astype(jnp.bfloat16)
            for r in range(2):
                acc = jnp.zeros((HALF, TILE), jnp.float32)
                for n in range(columns):
                    acc = acc - jnp.dot(
                        mixes[n], spread[n, r * HALF : r * HALF + TILE, :], preferred_element_type=jnp.float32
                    )
                total[r * HALF : (r + 1) * HALF, :] = acc

            @pl.when(q == 1)
            def _():
                start = pl.multiple_of(position * TILE, TILE)
                total[...] = total[...] + science[:, pl.ds(start, TILE)]

            total[...] = pltpu.roll(
                pltpu.roll(total[...], lax.rem(TILE - down, TILE), 0), lax.rem(TILE - right, TILE), 1
            )

            @pl.when(member == 1)
            def _():
                start = pl.multiple_of(RECORD + j * TILE, EDGE)
                total[...] = total[...] + from_chip[pl.ds(start, TILE), :].astype(jnp.float32)

            @pl.when(member == -1)
            def _():
                start = pl.multiple_of(NEAR_ROWS + j * TILE, EDGE)
                total[...] = total[...] + from_next[pl.ds(start, TILE), :].astype(jnp.float32)

            count = slot_of[SLOTS + k]
            share = jnp.float32(1.0)
            for n in range(2, SLOTS + 1):
                share = jnp.where(count == n, jnp.float32(1.0 / n), share)
            out[local] = out[local] + total[...] * share

        return carry

    lax.fori_loop(0, SLOTS, slot_step, 0)


def body(science, patches, margin, kernel_coef, ccd_first):
    strips = lax.axis_size("visit")
    owned = patches.shape[0]
    per_strip = science.shape[1] // TILE
    sizes = (strips, per_strip, owned)
    margin = margin.T
    smem = pl.BlockSpec(memory_space=pltpu.SMEM)
    vmem = pl.BlockSpec(memory_space=pltpu.VMEM)
    hbm = pl.BlockSpec(memory_space=pl.ANY)
    stays = pl.BlockSpec(memory_space=pltpu.HBM)
    bf16 = jnp.bfloat16
    f32 = jnp.float32
    aligned, to_chip, to_next, to_far = pl.pallas_call(
        functools.partial(pack_kernel, sizes),
        out_shape=(
            jax.ShapeDtypeStruct((SLOTS, TILE, TILE), bf16),
            jax.ShapeDtypeStruct((RECORD + CAP * TILE, TILE), bf16),
            jax.ShapeDtypeStruct((NEAR_ROWS + CAP * TILE, TILE), bf16),
            jax.ShapeDtypeStruct((PIECE_ROWS, TILE), bf16),
        ),
        in_specs=[stays] * 4,
        out_specs=(vmem, vmem, vmem, vmem),
        scratch_shapes=[
            pltpu.SMEM(margin.shape, jnp.int32),
            pltpu.VMEM(kernel_coef.shape[::-1], f32),
            pltpu.VMEM((SLOTS, TILE, TILE), f32),
            pltpu.VMEM((TILE, per_strip * TILE), f32),
            pltpu.SMEM((SLOTS,), jnp.int32),
            pltpu.SemaphoreType.DMA((SLOTS,)),
            pltpu.SemaphoreType.DMA,
            pltpu.SemaphoreType.DMA((2,)),
        ],
        compiler_params=pltpu.CompilerParams(vmem_limit_bytes=52 * 2**20),
        name="pack",
    )(margin, kernel_coef.T, patches, science)

    on_chip = [(i, i ^ 1) for i in range(strips)]
    next_chip = [p for i in range(1, strips - 1, 2) for p in ((i, i + 1), (i + 1, i))]
    far = [p for i in range(1, strips - 3, 2) for p in ((i, i + 3), (i + 3, i))]
    two = [p for i in range(0, strips - 2, 2) for p in ((i, i + 2), (i + 3, i + 1))]
    from_next = lax.ppermute(to_next, "visit", next_chip)
    from_two = lax.ppermute(to_chip[NEAR_ROWS:RECORD], "visit", two)
    from_far = lax.ppermute(to_far, "visit", far)
    from_chip = lax.ppermute(to_chip, "visit", on_chip)
    from_next, from_two, from_far, from_chip = lax.optimization_barrier((from_next, from_two, from_far, from_chip))
    relay = jnp.concatenate([from_next[:NEAR_ROWS], from_two], axis=0)
    from_across = lax.ppermute(relay, "visit", on_chip)

    columns = SIGMAS * ORDERS
    return pl.pallas_call(
        functools.partial(match_kernel, sizes),
        out_shape=jax.ShapeDtypeStruct(patches.shape, f32),
        in_specs=[smem, smem] + [vmem] * 8,
        out_specs=vmem,
        scratch_shapes=[
            pltpu.VMEM((7, RECORD, TILE), bf16),
            pltpu.VMEM((2, TILE + 2 * EDGE, TILE), bf16),
            pltpu.VMEM((columns, TILE + HALF, TILE), bf16),
            pltpu.VMEM((columns, HALF, TILE), bf16),
            pltpu.VMEM((columns, HALF, TILE), f32),
            pltpu.VMEM((TILE, columns * HALF), bf16),
            pltpu.VMEM((TILE, TILE), f32),
            pltpu.SMEM((2 * SLOTS,), jnp.int32),
        ],
        compiler_params=pltpu.CompilerParams(vmem_limit_bytes=24 * 2**20),
        name="match",
    )(margin, ccd_first, aligned, to_chip, from_chip, from_next, from_two, from_across, from_far, science)


def solution(mesh):
    in_specs = (
        P(("grp", "visit"), None),
        P(("grp", "visit"), None, None),
        P("grp", None),
        P(None, ("grp", "visit")),
        P("grp"),
    )
    out_specs = P(("grp", "visit"), None, None)
    return jax.shard_map(body, mesh=mesh, in_specs=in_specs, out_specs=out_specs, check_vma=False)
```

time: 46.2 us -> 33.2 us (0.72); the launches traced: 45.3 us -> 33 us
  waiting for transfers between devices: 11.4 us -> 2.79 us
  local copies, waits for them, and re-layouts: 4.63 us -> 1.48 us
  Pallas kernels: 16.9 us -> 14.9 us
  starting transfers between devices: 12.3 us -> 13.8 us
    ppermute x3, waiting for transfers between devices: 7.06 us -> 1.09 us  [the longest x1 1.08 us: body(): from_across = lax.ppermute(relay, 'visit', on_chip)]
    ppermute x1, starting transfers between devices: 2.08 us -> 4.33 us  [body(): from_far = lax.ppermute(to_far, 'visit', far)]
    ppermute x1, waiting for transfers between devices: 3.48 us -> 1.7 us  [body(): from_far = lax.ppermute(to_far, 'visit', far)]
    unnamed x12 -> x8, local copies, waits for them, and re-layouts: 2.97 us -> 1.46 us
    pallas_call x1, Pallas kernels: 4.83 us -> 3.73 us  [body(): pl.pallas_call(functools.partial(pack_kernel, sizes), out_shape=(jax.Shap...]
    slice x2, local copies, waits for them, and re-layouts: 0.95 us -> 0.02 us  [the longest x1 0.01 us: body(): relay = jnp.concatenate([from_next[:NEAR_ROWS], from_two], axis=0)]
    ppermute x1, waiting for transfers between devices: 0.9 us -> 0.01 us  [body(): from_chip = lax.ppermute(to_chip, 'visit', on_chip)]
    pallas_call x1, Pallas kernels: 12 us -> 11.1 us  [body(): pl.pallas_call(functools.partial(match_kernel, sizes), out_shape=jax.Shap...]
  transfers between devices with their start and end apart: 5 -> 5, of which waited for: 4 -> 2; matrix products, arithmetic and copies ran while one was open for 2% -> 0% of each run, Pallas kernels for 0% -> 0%
where the time goes in v1:
time: 33.2 us; the launch traced here: 33 us
  Pallas kernels  14.9 us (45%)
  starting transfers between devices  13.8 us (42%)
  waiting for transfers between devices  2.79 us (8%)
  local copies, waits for them, and re-layouts  1.48 us (4%)
    pallas_call x1, Pallas kernels, body(): pl.pallas_call(functools.partial(match_kernel, sizes), out_shape=jax.Shap...  11.1 us
    ppermute x1, starting transfers between devices, body(): from_far = lax.ppermute(to_far, 'visit', far)  4.33 us
    pallas_call x1, Pallas kernels, body(): pl.pallas_call(functools.partial(pack_kernel, sizes), out_shape=(jax.Shap...  3.73 us
    ppermute x1, starting transfers between devices, body(): from_across = lax.ppermute(relay, 'visit', on_chip)  3.7 us
    ppermute x1, starting transfers between devices, body(): from_next = lax.ppermute(to_next, 'visit', next_chip)  3.24 us
    ppermute x1, starting transfers between devices, body(): from_two = lax.ppermute(to_chip[NEAR_ROWS:RECORD], 'visit', two)  2.27 us
    ppermute x1, waiting for transfers between devices, body(): from_far = lax.ppermute(to_far, 'visit', far)  1.7 us
    unnamed x8, local copies, waits for them, and re-layouts  1.46 us
  transfers between devices with their start and end apart: 5, of which 2 were waited for; matrix products, arithmetic and copies ran while one was open for 0% of the time, Pallas kernels for 0%

profile of v1, /device:TPU:15, one launch (start us, length us, event | category | flops | bytes accessed | tf_op | source)
XLA Modules:
  0.0 33.0 jit_solution(12356566179294979208)
XLA Ops:
  0.0 0.0 copy-start
  0.0 0.0 copy-start.1
  0.0 0.8 %copy-done.1 = s32[64,3]{0,1:T(4,128)S(1)} copy-done((s32[64,3]{0,1:T(4,128)S(1)}, s32[64,3]{0,1:T(4,128)}, u32[]{:S(2)}) %copy-start.1) | copy-done | bytes 792
  0.8 0.0 copy-start.2
  0.8 0.7 %copy-done.2 = f32[27,4]{0,1:T(4,128)S(1)} copy-done((f32[27,4]{0,1:T(4,128)S(1)}, f32[27,4]{0,1:T(4,128)}, u32[]{:S(2)}) %copy-start.2) | copy-done | bytes 456
  1.5 0.0 copy-start.3
  1.5 3.7 %pack.1 = (bf16[6,256,256]{2,1,0:T(8,128)(2,1)S(1)}, bf16[912,256]{1,0:T(8,128)(2,1)S(1)}, bf16[784,256]{1,0:T(8,128)(2,1)S(1)}, bf16[32,256]{1,0:T(8,128)(2,1)S(1)}) custom-call(s32[3,64]{1,0:T(4,128)S(1)} %bitcast.2, f32[4,27]{1,0:T(4,128)S(1)} %bitcast.4, f32[8,256,256]{2,1,0:T(8,128)} %patches.1, f32[256,1024]{1,0:T(8,128)} %science.3), custom_call_target="tpu_custom_call" | custom-call | tf_op jit(solution)/shard_map/pack/pallas_call | solution.py:322
  5.2 0.2 collective-permute-start.3
  5.4 3.2 %collective-permute-start = (bf16[784,256]{1,0:T(8,128)(2,1)S(1)}, bf16[784,256]{1,0:T(8,128)(2,1)S(1)}, u32[]{:S(2)}, u32[]{:S(2)}) collective-permute-start(bf16[784,256]{1,0:T(8,128)(2,1)S(1)} %get-tuple-element.15), channel_id=1, source_target_pairs={{1,2},{2,1},{3,4},{4,3},{5,6},{6,5},{7,8},{8,7},{9,10},{10,9},{11,... | collective-permute-start | bytes 1204232 | tf_op jit(solution)/shard_map/ppermute | solution.py:350
  8.7 2.3 %collective-permute-start.1 = (bf16[128,256]{1,0:T(8,128)(2,1)S(1)}, bf16[128,256]{1,0:T(8,128)(2,1)S(1)}, u32[]{:S(2)}, u32[]{:S(2)}) collective-permute-start(bf16[128,256]{1,0:T(8,128)(2,1)S(1)} %slice.6), channel_id=1, source_target_pairs={{0,2},{3,1},{2,4},{5,3},{4,6},{7,5},{6,8},{9,7},{8,10},{11,9},{10,... | collective-permute-start | bytes 196616 | tf_op jit(solution)/shard_map/ppermute | solution.py:351
  11.0 4.3 %collective-permute-start.2 = (bf16[32,256]{1,0:T(8,128)(2,1)S(1)}, bf16[32,256]{1,0:T(8,128)(2,1)S(1)}, u32[]{:S(2)}, u32[]{:S(2)}) collective-permute-start(bf16[32,256]{1,0:T(8,128)(2,1)S(1)} %get-tuple-element.16), channel_id=1, source_target_pairs={{1,4},{4,1},{3,6},{6,3},{5,8},{8,5},{7,10},{10,7},{9,12},{12,9},{1... | collective-permute-start | bytes 49160 | tf_op jit(solution)/shard_map/ppermute | solution.py:352
  15.3 1.7 %collective-permute-done.2.from_far = bf16[32,256]{1,0:T(8,128)(2,1)S(1)} collective-permute-done((bf16[32,256]{1,0:T(8,128)(2,1)S(1)}, bf16[32,256]{1,0:T(8,128)(2,1)S(1)}, u32[]{:S(2)}, u32[]{:S(2)}) %collective-permute-start.2) | collective-permute-done | bytes 16416 | tf_op jit(solution)/shard_map/ppermute | solution.py:352
  17.0 0.0 collective-permute-done.1.from_two
  17.0 0.0 collective-permute-done.from_next
  17.0 0.0 collective-permute-done.3.from_chip
  17.1 3.7 %collective-permute-start.4 = (bf16[400,256]{1,0:T(8,128)(2,1)S(1)}, bf16[400,256]{1,0:T(8,128)(2,1)S(1)}, u32[]{:S(2)}, u32[]{:S(2)}) collective-permute-start(bf16[400,256]{1,0:T(8,128)(2,1)S(1)} %pad_maximum_fusion), channel_id=1, source_target_pairs={{0,1},{1,0},{2,3},{3,2},{4,5},{5,4},{6,7},{7,6},{8,9},{9,8},{10,11... | collective-permute-start | bytes 614408 | tf_op jit(solution)/shard_map/ppermute | solution.py:356
  20.8 1.1 %collective-permute-done.4.from_across = bf16[400,256]{1,0:T(8,128)(2,1)S(1)} collective-permute-done((bf16[400,256]{1,0:T(8,128)(2,1)S(1)}, bf16[400,256]{1,0:T(8,128)(2,1)S(1)}, u32[]{:S(2)}, u32[]{:S(2)}) %collective-permute-start.4) | collective-permute-done | bytes 204832 | tf_op jit(solution)/shard_map/ppermute | solution.py:356
  21.8 0.0 copy-done
  21.8 0.0 copy-done.3
  21.8 11.1 %match.1 = f32[8,256,256]{2,1,0:T(8,128)} custom-call(s32[3,64]{1,0:T(4,128)S(1)} %bitcast.3, s32[16]{0:T(128)S(1)} %copy-done.3, bf16[6,256,256]{2,1,0:T(8,128)(2,1)S(1)} %get-tuple-element.13.aligned, bf16[912,256]{1,0:T(8,128)(2,1)S(1)} %get-tuple-element.14.own_record, bf16[912,256]{1,0:T(8,128)(2,1)S(1)} %collective-permute-done.3.from_chip, ...), custom_call_target="tpu_custom_call" | custom-call | tf_op jit(solution)/shard_map/match/pallas_call | solution.py:359
  (3 shorter events, 0.0 us)
Async XLA Ops:
  0.0 21.8 %copy-start = (f32[256,1024]{1,0:T(8,128)S(1)}, f32[256,1024]{1,0:T(8,128)}, u32[]{:S(2)}) copy-start(f32[256,1024]{1,0:T(8,128)} %science.3) | copy-start | bytes 3145732
  0.0 0.8 %copy-start.1 = (s32[64,3]{0,1:T(4,128)S(1)}, s32[64,3]{0,1:T(4,128)}, u32[]{:S(2)}) copy-start(s32[64,3]{0,1:T(4,128)} %param.7) | copy-start | bytes 2308
  0.8 0.7 %copy-start.2 = (f32[27,4]{0,1:T(4,128)S(1)}, f32[27,4]{0,1:T(4,128)}, u32[]{:S(2)}) copy-start(f32[27,4]{0,1:T(4,128)} %param.8) | copy-start | bytes 1300
  1.5 20.4 %copy-start.3 = (s32[16]{0:T(128)S(1)}, s32[16]{0:T(128)}, u32[]{:S(2)}) copy-start(s32[16]{0:T(128)} %ccd_first.1) | copy-start | bytes 196
  5.2 11.8 %collective-permute-start.3 = (bf16[912,256]{1,0:T(8,128)(2,1)S(1)}, bf16[912,256]{1,0:T(8,128)(2,1)S(1)}, u32[]{:S(2)}, u32[]{:S(2)}) collective-permute-start(bf16[912,256]{1,0:T(8,128)(2,1)S(1)} %get-tuple-element.14.own_record), channel_id=1, source_target_pairs={{0,1},{1,0},{2,3},{3,2},{4,5},{5,4},{6,7},{7,6},{8,9},{9,8},{10,11... | collective-permute-start | bytes 1400840 | tf_op jit(solution)/shard_map/ppermute | solution.py:353
  5.4 11.6 %collective-permute-start = (bf16[784,256]{1,0:T(8,128)(2,1)S(1)}, bf16[784,256]{1,0:T(8,128)(2,1)S(1)}, u32[]{:S(2)}, u32[]{:S(2)}) collective-permute-start(bf16[784,256]{1,0:T(8,128)(2,1)S(1)} %get-tuple-element.15), channel_id=1, source_target_pairs={{1,2},{2,1},{3,4},{4,3},{5,6},{6,5},{7,8},{8,7},{9,10},{10,9},{11,... | collective-permute-start | bytes 1204232 | tf_op jit(solution)/shard_map/ppermute | solution.py:350
  8.7 8.3 %collective-permute-start.1 = (bf16[128,256]{1,0:T(8,128)(2,1)S(1)}, bf16[128,256]{1,0:T(8,128)(2,1)S(1)}, u32[]{:S(2)}, u32[]{:S(2)}) collective-permute-start(bf16[128,256]{1,0:T(8,128)(2,1)S(1)} %slice.6), channel_id=1, source_target_pairs={{0,2},{3,1},{2,4},{5,3},{4,6},{7,5},{6,8},{9,7},{8,10},{11,9},{10,... | collective-permute-start | bytes 196616 | tf_op jit(solution)/shard_map/ppermute | solution.py:351
  11.0 6.0 %collective-permute-start.2 = (bf16[32,256]{1,0:T(8,128)(2,1)S(1)}, bf16[32,256]{1,0:T(8,128)(2,1)S(1)}, u32[]{:S(2)}, u32[]{:S(2)}) collective-permute-start(bf16[32,256]{1,0:T(8,128)(2,1)S(1)} %get-tuple-element.16), channel_id=1, source_target_pairs={{1,4},{4,1},{3,6},{6,3},{5,8},{8,5},{7,10},{10,7},{9,12},{12,9},{1... | collective-permute-start | bytes 49160 | tf_op jit(solution)/shard_map/ppermute | solution.py:352
  17.1 4.8 %collective-permute-start.4 = (bf16[400,256]{1,0:T(8,128)(2,1)S(1)}, bf16[400,256]{1,0:T(8,128)(2,1)S(1)}, u32[]{:S(2)}, u32[]{:S(2)}) collective-permute-start(bf16[400,256]{1,0:T(8,128)(2,1)S(1)} %pad_maximum_fusion), channel_id=1, source_target_pairs={{0,1},{1,0},{2,3},{3,2},{4,5},{5,4},{6,7},{7,6},{8,9},{9,8},{10,11... | collective-permute-start | bytes 614408 | tf_op jit(solution)/shard_map/ppermute | solution.py:356
